TPU v7x, 32 devices: a whole 2x2x4 slice. The times are simulated.
32 devices in a mesh: fsdp: 4 (over y, x), ctx: 8 (over z, core).
Axes of the slice: x: 2, y: 2, z: 4, core: 2. Of those that a mesh axis runs over, the one named last changes fastest.
Arguments:
- tokens: bfloat16 [4096, 2048], P(('fsdp', 'ctx')), may hold values from -6 to 6
- w_qkv: bfloat16 [2048, 6144], P(('fsdp', 'ctx')), may hold values from -0.125 to 0.125
- w_out: bfloat16 [2048, 2048], P(('fsdp', 'ctx')), may hold values from -1 to 1
- w_gate_up: bfloat16 [2048, 16384], P(('fsdp', 'ctx')), may hold values from -0.125 to 0.125
- w_down: bfloat16 [8192, 2048], P(('fsdp', 'ctx')), may hold values from -0.0625 to 0.0625
- seq_lengths: int32 [4, 2], P('fsdp'), may hold values from 1 to 768, 1024 in all within a row
- block_order: int32 [4, 8], P('fsdp'), may hold values from 0 to 7, as said below
- cotangent: bfloat16 [4096, 2048], P(('fsdp', 'ctx')), may hold values from -6 to 6
Outputs:
- layer_out: bfloat16 [4096, 2048], P(('fsdp', 'ctx'))
- tokens_grad: float32 [4096, 2048], P(('fsdp', 'ctx'))
- qkv_grad: float32 [2048, 6144], P(('fsdp', 'ctx'))
- out_grad: float32 [2048, 2048], P(('fsdp', 'ctx'))
- gate_up_grad: float32 [2048, 16384], P(('fsdp', 'ctx'))
- down_grad: float32 [8192, 2048], P(('fsdp', 'ctx'))
Inputs may be any that keep to these rules, and one draw needn't show every extreme that they name: `seq_lengths`: the lengths of each group sum to 1024, and none is longer than 768. `block_order`: each row names every block of its group exactly once.
All inputs are finite; a program needn't handle non-finite values.
Results may differ from a plain program's by a relative error of at most 0.018.
Values may be sent and summed in bfloat16 or wider, within the bound.
A program may use at most 704 MiB of HBM per device.

v0:
```python
import jax
import jax.numpy as jnp
from jax import lax
from jax.sharding import PartitionSpec as P

HEADS = 16
HEAD_DIM = 128
BLOCK = 128


def normalize(values):
    average = jnp.mean(values, axis=-1, keepdims=True)
    centered = values - average
    variance = jnp.mean(centered * centered, axis=-1, keepdims=True)
    inv_root = lax.rsqrt(variance + 1e-05)
    return (centered * inv_root, inv_root)


def norm_back(upstream, normed, inv_root):
    first_mean = jnp.mean(upstream, axis=-1, keepdims=True)
    second_mean = jnp.mean(upstream * normed, axis=-1, keepdims=True)
    return inv_root * (upstream - first_mean - normed * second_mean)


def places(token_index, lengths):
    seq_ends = jnp.cumsum(lengths)
    sequence = jnp.sum((token_index[:, None] >= seq_ends[None, :]).astype(jnp.int32), axis=1)
    before = jnp.arange(lengths.shape[0], dtype=jnp.int32)
    seq_start = jnp.sum(jnp.where(before[None, :] < sequence[:, None], lengths[None, :], 0), axis=1)
    return (sequence, token_index - seq_start)


def initial_index(row_index, order_row):
    slot_index = row_index // BLOCK
    slot_table = jnp.arange(order_row.shape[0], dtype=jnp.int32)
    picked = jnp.sum(
        jnp.where(slot_table[None, :] == slot_index[:, None], order_row[None, :], 0), axis=1
    )
    return picked * BLOCK + row_index % BLOCK


def angle_tables(position):
    half_dim = HEAD_DIM // 2
    frequency = 10000.0 ** (-jnp.arange(half_dim, dtype=jnp.float32) * 2.0 / HEAD_DIM)
    angle_table = position.astype(jnp.float32)[:, None] * frequency[None, :]
    angle_table = jnp.concatenate([angle_table, angle_table], axis=-1)
    return (jnp.cos(angle_table)[:, None, :], jnp.sin(angle_table)[:, None, :])


def rotate(values, cosine_table, sine_table):
    half_dim = values.shape[-1] // 2
    turned = jnp.concatenate([-values[..., half_dim:], values[..., :half_dim]], axis=-1)
    return values * cosine_table + turned * sine_table


def unrotate(values, cosine_table, sine_table):
    half_dim = values.shape[-1] // 2
    scaled = values * sine_table
    turned = jnp.concatenate([scaled[..., half_dim:], -scaled[..., :half_dim]], axis=-1)
    return values * cosine_table + turned


def dot(left, right):
    return jnp.dot(left, right, preferred_element_type=jnp.float32)


def times_transposed(left, right):
    return lax.dot_general(
        left, right, (((1,), (1,)), ((), ())), preferred_element_type=jnp.float32
    )


def column_product(left, right):
    return lax.dot_general(
        left, right, (((0,), (0,)), ((), ())), preferred_element_type=jnp.float32
    )


def gather(values, axes):
    return lax.all_gather(values, axes, axis=0, tiled=True)


def scatter(values, axes):
    return lax.psum_scatter(values, axes, scatter_dimension=0, tiled=True)


def spread_columns(weight, outer, parts):
    rows, columns = weight.shape
    inner = columns // (outer * parts)
    pieces = weight.reshape(rows, outer, parts, inner).transpose(2, 0, 1, 3)
    pieces = lax.all_to_all(pieces, "ctx", split_axis=0, concat_axis=0, tiled=True)
    return pieces.reshape(parts * rows, outer * inner)


def collect_rows(grad, outer, parts):
    rows, columns = grad.shape
    inner = columns // outer
    pieces = grad.reshape(parts, rows // parts, columns)
    pieces = lax.all_to_all(pieces, "ctx", split_axis=0, concat_axis=0, tiled=True)
    pieces = pieces.reshape(parts, rows // parts, outer, inner).transpose(1, 2, 0, 3)
    return pieces.reshape(rows // parts, outer * parts * inner).astype(jnp.float32)


def per_device(tokens, w_qkv, w_out, w_gate_up, w_down, seq_lengths, block_order, cotangent):
    lengths = seq_lengths[0]
    order_row = block_order[0]
    parts = lax.axis_size("ctx")
    groups = lax.axis_size("fsdp")
    rows, width = tokens.shape
    length = rows * parts
    heads = HEADS // parts
    head_width = heads * HEAD_DIM
    low = jnp.bfloat16
    score_scale = HEAD_DIM ** (-0.5)
    qkv_cols = gather(spread_columns(w_qkv, 3, parts), "fsdp")
    out_full = gather(w_out, ("fsdp", "ctx"))
    gate_up_cols = gather(spread_columns(w_gate_up, 2 * groups, parts), "fsdp")
    down_rows = gather(w_down, "fsdp")
    cot_full = gather(cotangent, "ctx")
    inputs = tokens.astype(jnp.float32)
    normed_in, root_in = normalize(inputs)
    normed_in_full = gather(normed_in.astype(low), "ctx")
    row_index = jnp.arange(length, dtype=jnp.int32)
    seq, pos = places(initial_index(row_index, order_row), lengths)
    cosine_table, sine_table = angle_tables(pos)
    allowed = ((seq[:, None] == seq[None, :]) & (pos[None, :] <= pos[:, None]))[None]
    qkv = dot(normed_in_full, qkv_cols)
    head_shape = (length, heads, HEAD_DIM)
    queries = rotate(qkv[:, :head_width].reshape(head_shape), cosine_table, sine_table).astype(low)
    keys = rotate(
        qkv[:, head_width : 2 * head_width].reshape(head_shape), cosine_table, sine_table
    ).astype(low)
    values = qkv[:, 2 * head_width :].astype(low).reshape(head_shape)
    scores = jnp.einsum("qhd,khd->hqk", queries, keys, preferred_element_type=jnp.float32)
    scores = jnp.where(allowed, scores * score_scale, -1e30)
    row_max = jnp.max(scores, axis=-1)
    weights = jnp.where(allowed, jnp.exp(scores - row_max[..., None]), 0.0)
    row_total = jnp.sum(weights, axis=-1)
    mixed = jnp.einsum(
        "hqk,khd->qhd", weights.astype(low), values, preferred_element_type=jnp.float32
    )
    log_total = row_max + jnp.log(row_total)
    attn_heads = mixed / jnp.transpose(row_total)[..., None]
    mix_pieces = attn_heads.astype(low).reshape(parts, rows, head_width)
    mix_pieces = lax.all_to_all(mix_pieces, "ctx", split_axis=0, concat_axis=0, tiled=True)
    mix_low = mix_pieces.transpose(1, 0, 2).reshape(rows, width)
    residual = inputs + dot(mix_low, out_full)
    normed_mid, root_mid = normalize(residual)
    normed_mid_full = gather(normed_mid.astype(low), "ctx")
    gate_up = dot(normed_mid_full, gate_up_cols)
    units = gate_up.shape[1] // 2
    gate_part = gate_up[:, :units]
    up_part = gate_up[:, units:]
    sigmoid_gate = jax.nn.sigmoid(gate_part)
    silu_gate = gate_part * sigmoid_gate
    activated = (silu_gate * up_part).astype(low)
    down_out = scatter(dot(activated, down_rows).astype(low), "ctx")
    layer_out = (residual + down_out.astype(jnp.float32)).astype(low)
    down_grad = scatter(column_product(activated, cot_full).astype(low), "fsdp").astype(jnp.float32)
    act_grad = times_transposed(cot_full, down_rows)
    gate_grad = act_grad * up_part * sigmoid_gate * (1.0 + gate_part * (1.0 - sigmoid_gate))
    up_grad = act_grad * silu_gate
    gate_up_back = jnp.concatenate([gate_grad, up_grad], axis=1).astype(low)
    mid_back = scatter(times_transposed(gate_up_back, gate_up_cols).astype(low), "ctx")
    gate_up_grad = scatter(column_product(normed_mid_full, gate_up_back).astype(low), "fsdp")
    residual_back = cotangent.astype(jnp.float32) + norm_back(
        mid_back.astype(jnp.float32), normed_mid, root_mid
    )
    proj_back = residual_back.astype(low)
    mix_back = times_transposed(proj_back, out_full).astype(low)
    out_grad = scatter(column_product(mix_low, proj_back).astype(low), ("fsdp", "ctx"))
    back_pieces = mix_back.reshape(rows, parts, head_width).transpose(1, 0, 2)
    back_pieces = lax.all_to_all(back_pieces, "ctx", split_axis=0, concat_axis=0, tiled=True)
    back_heads = back_pieces.reshape(head_shape)
    delta = jnp.einsum("qhd,qhd->hq", back_heads.astype(jnp.float32), attn_heads)
    probs = jnp.where(allowed, jnp.exp(scores - log_total[..., None]), 0.0)
    value_back = jnp.einsum(
        "hqk,qhd->khd", probs.astype(low), back_heads, preferred_element_type=jnp.float32
    )
    prob_back = jnp.einsum("qhd,khd->hqk", back_heads, values, preferred_element_type=jnp.float32)
    score_back = (score_scale * probs * (prob_back - delta[..., None])).astype(low)
    query_back = jnp.einsum("hqk,khd->qhd", score_back, keys, preferred_element_type=jnp.float32)
    key_back = jnp.einsum("hqk,qhd->khd", score_back, queries, preferred_element_type=jnp.float32)
    qkv_back = jnp.concatenate(
        [
            unrotate(query_back, cosine_table, sine_table).reshape(length, head_width),
            unrotate(key_back, cosine_table, sine_table).reshape(length, head_width),
            value_back.reshape(length, head_width),
        ],
        axis=1,
    ).astype(low)
    in_back = scatter(times_transposed(qkv_back, qkv_cols).astype(low), "ctx")
    tokens_grad = residual_back + norm_back(in_back.astype(jnp.float32), normed_in, root_in)
    qkv_grad = scatter(column_product(normed_in_full, qkv_back).astype(low), "fsdp")
    return (
        layer_out,
        tokens_grad,
        collect_rows(qkv_grad, 3, parts),
        out_grad.astype(jnp.float32),
        collect_rows(gate_up_grad, 2 * groups, parts),
        down_grad,
    )


def solution(mesh):
    both = P(("fsdp", "ctx"), None)
    one = P("fsdp", None)
    return jax.shard_map(
        per_device,
        mesh=mesh,
        in_specs=(both, both, both, both, both, one, one, both),
        out_specs=(both,) * 6,
        check_vma=False,
    )
```

profile of v0, /device:TPU:0, one launch (start us, length us, event | category | flops | bytes accessed | tf_op | source)
XLA Modules:
  0.0 1039.7 jit_solution(7652950163884755804)
XLA Ops:
  7.2 1.3 copy.134
  8.7 27.2 %all_to_all.30 = bf16[8,64,3,256]{3,1,2,0:T(8,128)(2,1)S(1)} all-to-all(bf16[8,64,3,256]{3,1,2,0:T(8,128)(2,1)S(1)} %copy.97), channel_id=1, replica_groups=mesh['fsdp'=4,'ctx'=8] {'ctx'}, dimensions={0} | all-to-all | bytes 1572864 | tf_op jit(solution)/shard_map/all_to_all | solution.py:91
  36.6 1.0 copy.135
  39.0 1.1 fusion.20
  41.9 51.5 %all_to_all.31 = bf16[8,64,8,256]{3,2,1,0:T(8,128)(2,1)S(1)} all-to-all(bf16[8,64,8,256]{3,2,1,0:T(8,128)(2,1)S(1)} %bitcast.108), channel_id=1, replica_groups=mesh['fsdp'=4,'ctx'=8] {'ctx'}, dimensions={0} | all-to-all | bytes 4194304 | tf_op jit(solution)/shard_map/all_to_all | solution.py:91
  93.4 2.0 copy.138
  96.4 1.9 fusion.42
  98.3 1.2 compare_and_fusion
  99.5 30.2 %all-gather.8.cloned.1.call-done = bf16[1024,2048]{1,0:T(8,128)(2,1)} async-done(((bf16[128,2048]{1,0:T(8,128)(2,1)}), bf16[1024,2048]{1,0:T(8,128)(2,1)}) %all-gather.8.cloned.1.call-update) | async-done | bytes 4194320 | tf_op jit(solution)/shard_map/all_gather | solution.py:80
  129.7 6.2 fusion.73
  137.1 2.0 fusion.3
  139.2 2.3 fusion
  141.4 0.9 copy-done.3
  142.4 3.7 fusion.71
  146.3 23.3 %all_to_all.32 = bf16[8,128,256]{1,2,0:T(8,128)(2,1)S(1)} all-to-all(bf16[8,128,256]{1,2,0:T(8,128)(2,1)S(1)} %copy.102), channel_id=1, replica_groups=mesh['fsdp'=4,'ctx'=8] {'ctx'}, dimensions={0} | all-to-all | bytes 1048576 | tf_op jit(solution)/shard_map/all_to_all | solution.py:145
  169.6 40.8 %all-gather.12.cloned.1.call-done = bf16[2048,2048]{1,0:T(8,128)(2,1)} async-done(((bf16[64,2048]{1,0:T(8,128)(2,1)}), bf16[2048,2048]{1,0:T(8,128)(2,1)}) %all-gather.12.cloned.1.call-update) | async-done | bytes 8388624 | tf_op jit(solution)/shard_map/all_gather | solution.py:80
  210.4 4.7 fusion.72
  215.4 1.0 fusion.40
  218.4 80.4 %all-gather.16.cloned.1.call-done = bf16[2048,2048]{1,0:T(8,128)(2,1)} async-done(((bf16[512,2048]{1,0:T(8,128)(2,1)}), bf16[2048,2048]{1,0:T(8,128)(2,1)}) %all-gather.16.cloned.1.call-update) | async-done | bytes 8388624 | tf_op jit(solution)/shard_map/all_gather | solution.py:80
  298.8 48.9 %all-gather.14.cloned.1.call-done = bf16[1024,2048]{1,0:T(8,128)(2,1)} async-done(((bf16[128,2048]{1,0:T(8,128)(2,1)}), bf16[1024,2048]{1,0:T(8,128)(2,1)}) %all-gather.14.cloned.1.call-update) | async-done | bytes 4194320 | tf_op jit(solution)/shard_map/all_gather | solution.py:80
  347.7 14.5 %fusion.74 = f32[1024,2048]{1,0:T(8,128)} fusion(bf16[1024,2048]{1,0:T(8,128)(2,1)} %all-gather.14.cloned.1.call-done, bf16[2048,2048]{1,0:T(8,128)(2,1)} %all-gather.16.cloned.1.call-done), kind=kOutput, calls=%fused_computation.131 | convolution fusion | flops 8589934592 | bytes 20971520 | tf_op jit(solution)/shard_map/dot_general | solution.py:64
  362.3 38.6 %all-gather.18.cloned.1.call-done = bf16[1024,2048]{1,0:T(8,128)(2,1)} async-done(((bf16[256,2048]{1,0:T(8,128)(2,1)}), bf16[1024,2048]{1,0:T(8,128)(2,1)}) %all-gather.18.cloned.1.call-update) | async-done | bytes 4194320 | tf_op jit(solution)/shard_map/all_gather | solution.py:80
  400.8 48.5 %all-gather.20.cloned.1.call-done = bf16[1024,2048]{1,0:T(8,128)(2,1)} async-done(((bf16[128,2048]{1,0:T(8,128)(2,1)}), bf16[1024,2048]{1,0:T(8,128)(2,1)}) %all-gather.20.cloned.1.call-update) | async-done | bytes 4194320 | tf_op jit(solution)/shard_map/all_gather | solution.py:80
  449.3 13.1 %multiply_convert_fusion.2 = (bf16[1024,1024]{1,0:T(8,128)(2,1)S(1)}, bf16[1024,1024]{1,0:T(8,128)(2,1)S(1)}, bf16[1024,1024]{1,0:T(8,128)(2,1)}) fusion(f32[1024,2048]{1,0:T(8,128)} %fusion.74, bf16[1024,2048]{1,0:T(8,128)(2,1)} %all-gather.20.cloned.1.call-done, bf16[1024,2048]{1,0:T(8,128)(2,1)} %all-gather.18.cloned.1.call-done), kind=kOutput, calls=%fused_computation.12 | convolution fusion | flops 4310695936 | bytes 23068672 | tf_op jit(solution)/shard_map/dot_general | solution.py:68
  462.5 1.3 copy-done.24
  464.5 12.6 %convolution_convert_fusion.2 = bf16[1024,2048]{1,0:T(8,128)(2,1)} fusion(bf16[2048,2048]{1,0:T(8,128)(2,1)} %all-gather.16.cloned.1.call-done, bf16[1024,1024]{1,0:T(8,128)(2,1)S(1)} %get-tuple-element.13, bf16[1024,1024]{1,0:T(8,128)(2,1)S(1)} %get-tuple-element.12), kind=kOutput, calls=%fused_computation.21 | convolution fusion | flops 8600420352 | bytes 16777216 | tf_op jit(solution)/shard_map/dot_general | solution.py:68
  477.3 9.3 convolution_convert_fusion.5
  486.6 39.4 %reduce-scatter.10.cloned.1.call-done = bf16[128,2048]{1,0:T(8,128)(2,1)} async-done(((bf16[1024,2048]{1,0:T(8,128)(2,1)}), bf16[128,2048]{1,0:T(8,128)(2,1)}) %reduce-scatter.10.cloned.1.call-update) | async-done | bytes 524304 | tf_op jit(solution)/shard_map/reduce_scatter | solution.py:84
  526.0 1.4 convert_reduce_fusion.1
  527.4 49.3 %reduce-scatter.8.cloned.1.call-done = bf16[128,2048]{1,0:T(8,128)(2,1)} async-done(((bf16[1024,2048]{1,0:T(8,128)(2,1)}), bf16[128,2048]{1,0:T(8,128)(2,1)}) %reduce-scatter.8.cloned.1.call-update) | async-done | bytes 524304 | tf_op jit(solution)/shard_map/reduce_scatter | solution.py:84
  576.7 2.7 fusion.27
  579.4 7.1 convolution_convert_fusion.7
  586.4 2.1 copy.132
  588.6 4.2 all-to-all-start.3
  592.8 15.3 %all-to-all-done.3 = bf16[8,128,256]{1,2,0:T(8,128)(2,1)} async-done(((bf16[8,128,256]{1,2,0:T(8,128)(2,1)}), bf16[8,128,256]{1,2,0:T(8,128)(2,1)}, u32[]{:S(2)}, u32[]{:S(2)}) %all-to-all-start.3) | async-done | bytes 524320 | tf_op jit(solution)/shard_map/all_to_all | solution.py:173
  608.1 2.2 copy.107
  610.2 2.1 reshape.327
  612.3 1.5 fusion.36
  613.8 6.5 fusion.14
  620.4 6.2 multiply_convert_fusion
  626.7 1.5 convolution_bitcast_fusion
  628.2 0.9 broadcast_multiply_fusion.1
  631.5 4.9 convolution_convert_fusion.6
  636.7 14.0 %convolution_convert_fusion = bf16[2048,2048]{1,0:T(8,128)(2,1)} fusion(bf16[1024,2048]{1,0:T(8,128)(2,1)} %all-gather.14.cloned.1.call-done, bf16[1024,1024]{1,0:T(8,128)(2,1)} %copy-done.25, bf16[1024,1024]{1,0:T(8,128)(2,1)} %copy-done.24), kind=kOutput, calls=%fused_computation.4 | convolution fusion | flops 8602517504 | bytes 16777216 | tf_op jit(solution)/shard_map/dot_general | solution.py:74
  650.8 9.6 convolution_convert_fusion.4
  660.8 7.6 convolution_convert_fusion.3
  668.5 5.6 convolution_convert_fusion.1
  674.1 5.3 reduce-scatter.14.cloned.1.call-done
  679.4 4.6 all-to-all-start.4
  684.0 84.8 %reduce-scatter.18.cloned.1.call-done = bf16[512,2048]{1,0:T(8,128)(2,1)} async-done(((bf16[2048,2048]{1,0:T(8,128)(2,1)}), bf16[512,2048]{1,0:T(8,128)(2,1)}) %reduce-scatter.18.cloned.1.call-update) | async-done | bytes 2097168 | tf_op jit(solution)/shard_map/reduce_scatter | solution.py:84
  768.8 4.8 all-to-all-start.5
  773.6 50.6 %reduce-scatter.20.cloned.1.call-done = bf16[256,2048]{1,0:T(8,128)(2,1)} async-done(((bf16[1024,2048]{1,0:T(8,128)(2,1)}), bf16[256,2048]{1,0:T(8,128)(2,1)}) %reduce-scatter.20.cloned.1.call-update) | async-done | bytes 1048592 | tf_op jit(solution)/shard_map/reduce_scatter | solution.py:84
  824.3 2.8 convert_element_type.151
  827.0 1.9 reshape.335
  828.9 2.5 copy.114
  831.4 1.6 copy.139
  833.0 44.0 %reduce-scatter.12.cloned.1.call-done = bf16[128,2048]{1,0:T(8,128)(2,1)} async-done(((bf16[1024,2048]{1,0:T(8,128)(2,1)}), bf16[128,2048]{1,0:T(8,128)(2,1)}) %reduce-scatter.12.cloned.1.call-update) | async-done | bytes 524304 | tf_op jit(solution)/shard_map/reduce_scatter | solution.py:84
  877.1 1.4 convert_reduce_fusion
  878.5 2.5 fusion.23
  881.0 2.1 copy.140
  883.1 2.4 copy.115
  885.5 4.4 copy.141
  889.9 141.4 %reduce-scatter.16.cloned.1.call-done = bf16[64,2048]{1,0:T(8,128)(2,1)} async-done(((bf16[2048,2048]{1,0:T(8,128)(2,1)}), bf16[64,2048]{1,0:T(8,128)(2,1)}) %reduce-scatter.16.cloned.1.call-update) | async-done | bytes 262160 | tf_op jit(solution)/shard_map/reduce_scatter | solution.py:84
  1031.2 1.8 convert_element_type.144
  (115 shorter events, 12.6 us)
Async XLA Ops:
  7.2 92.3 %all-gather.10.cloned.1.call-start = ((), (), s32[]{:S(2)}) async-start(), calls=%async_computation.14 | async-start | bytes 3932160 | tf_op jit(solution)/shard_map/all_gather | solution.py:80
  8.5 29.2 %copy-start = (bf16[128,2048]{1,0:T(8,128)(2,1)S(1)}, bf16[128,2048]{1,0:T(8,128)(2,1)}, u32[]{:S(2)}) copy-start(bf16[128,2048]{1,0:T(8,128)(2,1)} %param.8) | copy-start | bytes 1572868
  8.7 32.2 %copy-start.11 = (bf16[64,16384]{1,0:T(8,128)(2,1)S(1)}, bf16[64,16384]{1,0:T(8,128)(2,1)}, u32[]{:S(2)}) copy-start(bf16[64,16384]{1,0:T(8,128)(2,1)} %param.11) | copy-start | bytes 6291460
  37.7 92.0 %all-gather.8.cloned.1.call-start = ((), (), s32[]{:S(2)}) async-start(), calls=%async_computation.13 | async-start | bytes 4718592 | tf_op jit(solution)/shard_map/all_gather | solution.py:80
  37.9 0.6 copy-start.16
  38.5 0.5 copy-start.18
  40.2 170.3 %all-gather.12.cloned.1.call-start = ((), (), s32[]{:S(2)}) async-start(), calls=%async_computation.15 | async-start | bytes 8650752 | tf_op jit(solution)/shard_map/all_gather | solution.py:80
  40.9 257.9 %all-gather.16.cloned.1.call-start = ((), (), s32[]{:S(2)}) async-start(), calls=%async_computation.17 | async-start | bytes 10485760 | tf_op jit(solution)/shard_map/all_gather | solution.py:80
  93.4 2.4 copy-start.21
  93.4 2.6 copy-start.20
  95.5 252.3 %all-gather.14.cloned.1.call-start = ((), (), s32[]{:S(2)}) async-start(), calls=%async_computation.16 | async-start | bytes 4718592 | tf_op jit(solution)/shard_map/all_gather | solution.py:80
  98.3 38.2 %copy-start.1 = (f32[1024,128]{0,1:T(8,128)}, f32[1024,128]{0,1:T(8,128)S(1)}, u32[]{:S(2)}) copy-start(f32[1024,128]{0,1:T(8,128)S(1)} %get-tuple-element.34) | copy-start | bytes 1572868
  98.3 38.2 %copy-start.4 = (f32[1024,128]{0,1:T(8,128)}, f32[1024,128]{0,1:T(8,128)S(1)}, u32[]{:S(2)}) copy-start(f32[1024,128]{0,1:T(8,128)S(1)} %get-tuple-element.33) | copy-start | bytes 1572868
  99.5 42.0 %copy-start.6 = (pred[1024,1024]{0,1:T(8,128)(4,1)}, pred[1024,1024]{0,1:T(8,128)(4,1)S(1)}, u32[]{:S(2)}) copy-start(pred[1024,1024]{0,1:T(8,128)(4,1)S(1)} %compare_and_fusion) | copy-start | bytes 3145732
  136.0 5.4 copy-start.14
  137.1 2.0 copy-start.8
  137.1 2.0 copy-start.12
  139.2 3.2 copy-start.3
  216.4 184.4 %all-gather.18.cloned.1.call-start = ((), (), s32[]{:S(2)}) async-start(), calls=%async_computation.18 | async-start | bytes 5242880 | tf_op jit(solution)/shard_map/all_gather | solution.py:80
  217.0 232.3 %all-gather.20.cloned.1.call-start = ((), (), s32[]{:S(2)}) async-start(), calls=%async_computation.20 | async-start | bytes 4718592 | tf_op jit(solution)/shard_map/all_gather | solution.py:80
  217.8 308.2 %reduce-scatter.10.cloned.1.call-start = ((), (), s32[]{:S(2)}) async-start(), calls=%async_computation.21 | async-start | bytes 4718592 | tf_op jit(solution)/shard_map/reduce_scatter | solution.py:84
  462.5 1.4 copy-start.24
  462.5 2.0 copy-start.25
  477.1 99.6 %reduce-scatter.8.cloned.1.call-start = ((), (), s32[]{:S(2)}) async-start(), calls=%async_computation.19 | async-start | bytes 4718592 | tf_op jit(solution)/shard_map/reduce_scatter | solution.py:84
  586.4 27.4 %copy-start.7 = (pred[1024,1024]{0,1:T(8,128)(4,1)S(1)}, pred[1024,1024]{0,1:T(8,128)(4,1)}, u32[]{:S(2)}) copy-start(pred[1024,1024]{0,1:T(8,128)(4,1)} %copy-done.6) | copy-start | bytes 3145732
  588.6 19.5 %all-to-all-start.3 = ((bf16[8,128,256]{1,2,0:T(8,128)(2,1)}), bf16[8,128,256]{1,2,0:T(8,128)(2,1)}, u32[]{:S(2)}, u32[]{:S(2)}) async-start(bf16[8,128,256]{1,2,0:T(8,128)(2,1)} %bitcast.118), calls=%async_computation.5 | async-start | bytes 1048576 | tf_op jit(solution)/shard_map/all_to_all | solution.py:173
  592.7 86.6 %reduce-scatter.14.cloned.1.call-start = ((), (), s32[]{:S(2)}) async-start(), calls=%async_computation.23 | async-start | bytes 3932160 | tf_op jit(solution)/shard_map/reduce_scatter | solution.py:84
  613.8 6.6 copy-start.10
  613.8 6.6 copy-start.15
  620.4 10.4 copy-start.23
  620.4 6.2 copy-start.13
  626.6 1.6 copy-start.2
  626.6 1.6 copy-start.9
  629.1 1.0 copy-start.5
  629.2 2.3 copy-start.22
  636.4 132.4 %reduce-scatter.18.cloned.1.call-start = ((), (), s32[]{:S(2)}) async-start(), calls=%async_computation.25 | async-start | bytes 10485760 | tf_op jit(solution)/shard_map/reduce_scatter | solution.py:84
  650.7 173.5 %reduce-scatter.20.cloned.1.call-start = ((), (), s32[]{:S(2)}) async-start(), calls=%async_computation.26 | async-start | bytes 5242880 | tf_op jit(solution)/shard_map/reduce_scatter | solution.py:84
  660.3 216.7 %reduce-scatter.12.cloned.1.call-start = ((), (), s32[]{:S(2)}) async-start(), calls=%async_computation.22 | async-start | bytes 4718592 | tf_op jit(solution)/shard_map/reduce_scatter | solution.py:84
  668.4 362.8 %reduce-scatter.16.cloned.1.call-start = ((), (), s32[]{:S(2)}) async-start(), calls=%async_computation.24 | async-start | bytes 8650752 | tf_op jit(solution)/shard_map/reduce_scatter | solution.py:84
  679.4 89.4 %all-to-all-start.4 = ((bf16[8,64,768]{2,1,0:T(8,128)(2,1)}), bf16[8,64,768]{2,1,0:T(8,128)(2,1)S(1)}, u32[]{:S(2)}, u32[]{:S(2)}) async-start(bf16[8,64,768]{2,1,0:T(8,128)(2,1)} %bitcast.122), calls=%async_computation.8 | async-start | bytes 1572864 | tf_op jit(solution)/shard_map/all_to_all | solution.py:99
  768.8 112.2 %all-to-all-start.5 = ((bf16[8,64,2048]{2,1,0:T(8,128)(2,1)}), bf16[8,64,2048]{2,1,0:T(8,128)(2,1)}, u32[]{:S(2)}, u32[]{:S(2)}) async-start(bf16[8,64,2048]{2,1,0:T(8,128)(2,1)} %bitcast.117), calls=%async_computation.11 | async-start | bytes 4194304 | tf_op jit(solution)/shard_map/all_to_all | solution.py:99
  827.0 50.0 %copy-start.17 = (f32[128]{0:T(128)S(1)}, f32[128]{0:T(128)}, u32[]{:S(2)}) copy-start(f32[128]{0:T(128)} %copy-done.16) | copy-start | bytes 1540
  827.0 50.0 %copy-start.19 = (f32[128]{0:T(128)S(1)}, f32[128]{0:T(128)}, u32[]{:S(2)}) copy-start(f32[128]{0:T(128)} %copy-done.18) | copy-start | bytes 1540
Sparse Core Ops, SparseCore 0:
  37.8 42.7 all-gather.9
  82.8 46.8 all-gather.7
  132.7 77.6 all-gather.11
  212.7 86.0 all-gather.15
  300.8 46.8 all-gather.13
  349.4 51.3 all-gather.17
  402.4 46.8 all-gather.19
  477.2 48.7 reduce-scatter.9
  528.3 48.3 reduce-scatter.7
  636.5 42.7 reduce-scatter.13
  682.4 86.3 reduce-scatter.17
  771.6 52.5 reduce-scatter.19
  827.1 49.8 reduce-scatter.11
  879.2 151.9 reduce-scatter.15
where the time goes:
time: 1040 us
  waiting for transfers between devices  720 us (69%)
  matrix products  130 us (12%)
  blocking collectives  102 us (10%)
  local copies, waits for them, and re-layouts  33.2 us (3%)
  other arithmetic  24.4 us (2%)
  starting transfers between devices  15.8 us (2%)
  between operations  14.7 us (1%)
    reduce_scatter x7, waiting for transfers between devices, scatter(): return lax.psum_scatter(values, axes, scatter_dimension=0, tiled=True)  415 us
    all_gather x7, waiting for transfers between devices, gather(): return lax.all_gather(values, axes, axis=0, tiled=True)  287 us
    all_to_all x2, blocking collectives, spread_columns(): lax.all_to_all(pieces, 'ctx', split_axis=0, concat_axis=0, tiled=True)  78.7 us
    dot_general x4, matrix products, times_transposed(): lax.dot_general(left, right, (((1,), (1,)), ((), ())), preferred_element_...  40.4 us
    dot_general x4, matrix products, dot(): return jnp.dot(left, right, preferred_element_type=jnp.float32)  34.8 us
    dot_general x4, matrix products, column_product(): lax.dot_general(left, right, (((0,), (0,)), ((), ())), preferred_element_...  34 us
    all_to_all x1, blocking collectives, per_device(): lax.all_to_all(mix_pieces, 'ctx', split_axis=0, concat_axis=0, tiled=True)  23.3 us
  transfers between devices with their start and end apart: 17, of which 14 were waited for; matrix products, arithmetic and copies ran while one was open for 11% of the time, Pallas kernels for 0%

commit v1 on v0

--- a/solution.py
+++ b/solution.py
@@ -2,10 +2,22 @@
 import jax.numpy as jnp
 from jax import lax
 from jax.sharding import PartitionSpec as P
+from jax.lax import axis_index, axis_size, ppermute
 
 HEADS = 16
 HEAD_DIM = 128
 BLOCK = 128
+
+
+def _try_all_fields(body, dim_at, local_block):
+    p_next, odd = (body.shape[:dim_at], body.shape[dim_at + 1 :])
+    return jnp.moveaxis(body.reshape(*p_next, local_block, -1, *odd), dim_at, 0)
+
+
+def lift_files_up(work_x, d_out):
+    work_x = jnp.moveaxis(work_x, 0, d_out)
+    h_now = work_x.shape
+    return work_x.reshape(*h_now[:d_out], h_now[d_out] * h_now[d_out + 1], *h_now[d_out + 2 :])
 
 
 def normalize(values):
@@ -142,7 +154,16 @@
     log_total = row_max + jnp.log(row_total)
     attn_heads = mixed / jnp.transpose(row_total)[..., None]
     mix_pieces = attn_heads.astype(low).reshape(parts, rows, head_width)
-    mix_pieces = lax.all_to_all(mix_pieces, "ctx", split_axis=0, concat_axis=0, tiled=True)
+    view_out, current_block = (axis_size("ctx"), axis_index("ctx"))
+    s_next = _try_all_fields(mix_pieces, 0, view_out)
+    chunks = [s_next[current_block]]
+    for u in range(1, view_out):
+        state_now = s_next[(current_block + u) % view_out]
+        chunks.append(
+            ppermute(state_now, "ctx", [(i0, (i0 + u) % view_out) for i0 in range(view_out)])
+        )
+    s_next = jnp.stack(chunks)[(current_block - jnp.arange(view_out)) % view_out]
+    mix_pieces = lift_files_up(s_next, 0)
     mix_low = mix_pieces.transpose(1, 0, 2).reshape(rows, width)
     residual = inputs + dot(mix_low, out_full)
     normed_mid, root_mid = normalize(residual)

time: 1040 us -> 1040 us (level)
  blocking collectives: 102 us -> 78.7 us
  starting transfers between devices: 15.8 us -> 32.3 us
    all_to_all x1 -> x0, blocking collectives: 23.3 us -> none  [per_device(): lax.all_to_all(mix_pieces, 'ctx', split_axis=0, concat_axis=0, tiled=True)]
    ppermute x0 -> x7, starting transfers between devices: none -> 16.9 us  [per_device(): ppermute(state_now, 'ctx', [(i0, (i0 + u) % view_out) for i0 in range(vie...]
  transfers between devices with their start and end apart: 17 -> 24, of which waited for: 14 -> 17; matrix products, arithmetic and copies ran while one was open for 11% -> 11% of each run, Pallas kernels for 0% -> 0%
where the time goes in v1:
time: 1040 us
  waiting for transfers between devices  723 us (70%)
  matrix products  130 us (12%)
  blocking collectives  78.7 us (8%)
  local copies, waits for them, and re-layouts  36 us (3%)
  starting transfers between devices  32.3 us (3%)
  other arithmetic  24.4 us (2%)
  between operations  15 us (1%)
    reduce_scatter x7, waiting for transfers between devices, scatter(): return lax.psum_scatter(values, axes, scatter_dimension=0, tiled=True)  414 us
    all_gather x7, waiting for transfers between devices, gather(): return lax.all_gather(values, axes, axis=0, tiled=True)  286 us
    all_to_all x2, blocking collectives, spread_columns(): lax.all_to_all(pieces, 'ctx', split_axis=0, concat_axis=0, tiled=True)  78.7 us
    dot_general x4, matrix products, times_transposed(): lax.dot_general(left, right, (((1,), (1,)), ((), ())), preferred_element_...  40.4 us
    dot_general x4, matrix products, dot(): return jnp.dot(left, right, preferred_element_type=jnp.float32)  34.8 us
    dot_general x4, matrix products, column_product(): lax.dot_general(left, right, (((0,), (0,)), ((), ())), preferred_element_...  34 us
  transfers between devices with their start and end apart: 24, of which 17 were waited for; matrix products, arithmetic and copies ran while one was open for 11% of the time, Pallas kernels for 0%

profile of v1, /device:TPU:0, one launch (start us, length us, event | category | flops | bytes accessed | tf_op | source)
XLA Modules:
  0.0 1039.5 jit_solution(6426174295951111515)
XLA Ops:
  7.2 1.3 copy.217
  8.7 27.2 %all_to_all.25 = bf16[8,64,3,256]{3,1,2,0:T(8,128)(2,1)S(1)} all-to-all(bf16[8,64,3,256]{3,1,2,0:T(8,128)(2,1)S(1)} %copy.157), channel_id=1, replica_groups=mesh['fsdp'=4,'ctx'=8] {'ctx'}, dimensions={0} | all-to-all | bytes 1572864 | tf_op jit(solution)/shard_map/all_to_all | solution.py:103
  41.8 51.5 %all_to_all.26 = bf16[8,64,8,256]{3,2,1,0:T(8,128)(2,1)S(1)} all-to-all(bf16[8,64,8,256]{3,2,1,0:T(8,128)(2,1)S(1)} %bitcast.146), channel_id=1, replica_groups=mesh['fsdp'=4,'ctx'=8] {'ctx'}, dimensions={0} | all-to-all | bytes 4194304 | tf_op jit(solution)/shard_map/all_to_all | solution.py:103
  93.3 2.0 copy.221
  96.5 1.9 fusion.42
  98.4 1.2 compare_and_fusion
  99.6 30.1 %all-gather.8.cloned.1.call-done = bf16[1024,2048]{1,0:T(8,128)(2,1)} async-done(((bf16[128,2048]{1,0:T(8,128)(2,1)}), bf16[1024,2048]{1,0:T(8,128)(2,1)}) %all-gather.8.cloned.1.call-update) | async-done | bytes 4194320 | tf_op jit(solution)/shard_map/all_gather | solution.py:92
  129.7 6.2 fusion.75
  137.1 2.0 fusion.3
  139.2 2.3 fusion
  142.4 3.7 fusion.73
  146.2 1.2 constant_dynamic-slice_fusion.7
  148.4 1.4 collective-permute-start.5
  150.5 1.2 collective-permute-start.2
  151.7 2.6 collective-permute-start.3
  156.7 11.0 %collective-permute-start.6 = (bf16[1,128,256]{2,1,0:T(8,128)(2,1)S(1)}, bf16[1,128,256]{2,1,0:T(8,128)(2,1)S(1)}, u32[]{:S(2)}, u32[]{:S(2)}) collective-permute-start(bf16[1,128,256]{2,1,0:T(8,128)(2,1)S(1)} %bitcast.170), channel_id=1, source_target_pairs={{0,7},{1,0},{2,1},{3,2},{4,3},{5,4},{6,5},{7,6},{8,15},{9,8},{10,9... | collective-permute-start | bytes 196616 | tf_op jit(solution)/shard_map/ppermute | solution.py:163
  167.8 2.7 collective-permute-done.6
  171.4 38.9 %all-gather.12.cloned.1.call-done = bf16[2048,2048]{1,0:T(8,128)(2,1)} async-done(((bf16[64,2048]{1,0:T(8,128)(2,1)}), bf16[2048,2048]{1,0:T(8,128)(2,1)}) %all-gather.12.cloned.1.call-update) | async-done | bytes 8388624 | tf_op jit(solution)/shard_map/all_gather | solution.py:92
  210.2 4.7 fusion.74
  217.6 81.0 %all-gather.16.cloned.1.call-done = bf16[2048,2048]{1,0:T(8,128)(2,1)} async-done(((bf16[512,2048]{1,0:T(8,128)(2,1)}), bf16[2048,2048]{1,0:T(8,128)(2,1)}) %all-gather.16.cloned.1.call-update) | async-done | bytes 8388624 | tf_op jit(solution)/shard_map/all_gather | solution.py:92
  298.6 48.9 %all-gather.14.cloned.1.call-done = bf16[1024,2048]{1,0:T(8,128)(2,1)} async-done(((bf16[128,2048]{1,0:T(8,128)(2,1)}), bf16[1024,2048]{1,0:T(8,128)(2,1)}) %all-gather.14.cloned.1.call-update) | async-done | bytes 4194320 | tf_op jit(solution)/shard_map/all_gather | solution.py:92
  347.6 14.5 %fusion.76 = f32[1024,2048]{1,0:T(8,128)} fusion(bf16[1024,2048]{1,0:T(8,128)(2,1)} %all-gather.14.cloned.1.call-done, bf16[2048,2048]{1,0:T(8,128)(2,1)} %all-gather.16.cloned.1.call-done), kind=kOutput, calls=%fused_computation.155 | convolution fusion | flops 8589934592 | bytes 20971520 | tf_op jit(solution)/shard_map/dot_general | solution.py:76
  362.1 38.6 %all-gather.18.cloned.1.call-done = bf16[1024,2048]{1,0:T(8,128)(2,1)} async-done(((bf16[256,2048]{1,0:T(8,128)(2,1)}), bf16[1024,2048]{1,0:T(8,128)(2,1)}) %all-gather.18.cloned.1.call-update) | async-done | bytes 4194320 | tf_op jit(solution)/shard_map/all_gather | solution.py:92
  400.7 48.5 %all-gather.20.cloned.1.call-done = bf16[1024,2048]{1,0:T(8,128)(2,1)} async-done(((bf16[128,2048]{1,0:T(8,128)(2,1)}), bf16[1024,2048]{1,0:T(8,128)(2,1)}) %all-gather.20.cloned.1.call-update) | async-done | bytes 4194320 | tf_op jit(solution)/shard_map/all_gather | solution.py:92
  449.2 13.1 %multiply_convert_fusion.2 = (bf16[1024,1024]{1,0:T(8,128)(2,1)S(1)}, bf16[1024,1024]{1,0:T(8,128)(2,1)S(1)}, bf16[1024,1024]{1,0:T(8,128)(2,1)}) fusion(f32[1024,2048]{1,0:T(8,128)} %fusion.76, bf16[1024,2048]{1,0:T(8,128)(2,1)} %all-gather.20.cloned.1.call-done, bf16[1024,2048]{1,0:T(8,128)(2,1)} %all-gather.18.cloned.1.call-done), kind=kOutput, calls=%fused_computation.13 | convolution fusion | flops 4310695936 | bytes 23068672 | tf_op jit(solution)/shard_map/dot_general | solution.py:80
  462.3 1.4 copy-done.24
  464.3 12.6 %convolution_convert_fusion.2 = bf16[1024,2048]{1,0:T(8,128)(2,1)} fusion(bf16[2048,2048]{1,0:T(8,128)(2,1)} %all-gather.16.cloned.1.call-done, bf16[1024,1024]{1,0:T(8,128)(2,1)S(1)} %get-tuple-element.13, bf16[1024,1024]{1,0:T(8,128)(2,1)S(1)} %get-tuple-element.12), kind=kOutput, calls=%fused_computation.22 | convolution fusion | flops 8600420352 | bytes 16777216 | tf_op jit(solution)/shard_map/dot_general | solution.py:80
  477.4 9.3 convolution_convert_fusion.5
  486.7 39.1 %reduce-scatter.10.cloned.1.call-done = bf16[128,2048]{1,0:T(8,128)(2,1)} async-done(((bf16[1024,2048]{1,0:T(8,128)(2,1)}), bf16[128,2048]{1,0:T(8,128)(2,1)}) %reduce-scatter.10.cloned.1.call-update) | async-done | bytes 524304 | tf_op jit(solution)/shard_map/reduce_scatter | solution.py:96
  525.8 1.4 convert_reduce_fusion.1
  527.2 49.3 %reduce-scatter.8.cloned.1.call-done = bf16[128,2048]{1,0:T(8,128)(2,1)} async-done(((bf16[1024,2048]{1,0:T(8,128)(2,1)}), bf16[128,2048]{1,0:T(8,128)(2,1)}) %reduce-scatter.8.cloned.1.call-update) | async-done | bytes 524304 | tf_op jit(solution)/shard_map/reduce_scatter | solution.py:96
  576.5 2.7 fusion.27
  579.2 7.1 convolution_convert_fusion.7
  586.3 2.1 copy.207
  588.4 4.2 all-to-all-start.2
  592.6 15.3 %all-to-all-done.2 = bf16[8,128,256]{1,2,0:T(8,128)(2,1)} async-done(((bf16[8,128,256]{1,2,0:T(8,128)(2,1)}), bf16[8,128,256]{1,2,0:T(8,128)(2,1)}, u32[]{:S(2)}, u32[]{:S(2)}) %all-to-all-start.2) | async-done | bytes 524320 | tf_op jit(solution)/shard_map/all_to_all | solution.py:194
  607.9 2.2 copy.182
  610.1 2.1 reshape.376
  612.1 1.5 fusion.36
  613.7 6.5 fusion.14
  620.2 6.2 multiply_convert_fusion
  626.5 1.5 convolution_bitcast_fusion
  631.3 4.9 convolution_convert_fusion.6
  636.5 14.0 %convolution_convert_fusion = bf16[2048,2048]{1,0:T(8,128)(2,1)} fusion(bf16[1024,2048]{1,0:T(8,128)(2,1)} %all-gather.14.cloned.1.call-done, bf16[1024,1024]{1,0:T(8,128)(2,1)} %copy-done.25, bf16[1024,1024]{1,0:T(8,128)(2,1)} %copy-done.24), kind=kOutput, calls=%fused_computation.5 | convolution fusion | flops 8602517504 | bytes 16777216 | tf_op jit(solution)/shard_map/dot_general | solution.py:86
  650.5 9.6 convolution_convert_fusion.4
  660.4 7.6 convolution_convert_fusion.3
  668.0 5.6 convolution_convert_fusion.1
  673.7 5.5 reduce-scatter.14.cloned.1.call-done
  679.1 4.6 all-to-all-start.3
  683.7 84.8 %reduce-scatter.18.cloned.1.call-done = bf16[512,2048]{1,0:T(8,128)(2,1)} async-done(((bf16[2048,2048]{1,0:T(8,128)(2,1)}), bf16[512,2048]{1,0:T(8,128)(2,1)}) %reduce-scatter.18.cloned.1.call-update) | async-done | bytes 2097168 | tf_op jit(solution)/shard_map/reduce_scatter | solution.py:96
  768.5 4.9 all-to-all-start.4
  773.4 50.6 %reduce-scatter.20.cloned.1.call-done = bf16[256,2048]{1,0:T(8,128)(2,1)} async-done(((bf16[1024,2048]{1,0:T(8,128)(2,1)}), bf16[256,2048]{1,0:T(8,128)(2,1)}) %reduce-scatter.20.cloned.1.call-update) | async-done | bytes 1048592 | tf_op jit(solution)/shard_map/reduce_scatter | solution.py:96
  824.0 2.8 convert_element_type.151
  826.8 1.9 reshape.384
  828.7 2.5 copy.189
  831.2 1.6 copy.222
  832.8 44.0 %reduce-scatter.12.cloned.1.call-done = bf16[128,2048]{1,0:T(8,128)(2,1)} async-done(((bf16[1024,2048]{1,0:T(8,128)(2,1)}), bf16[128,2048]{1,0:T(8,128)(2,1)}) %reduce-scatter.12.cloned.1.call-update) | async-done | bytes 524304 | tf_op jit(solution)/shard_map/reduce_scatter | solution.py:96
  876.8 1.4 convert_reduce_fusion
  878.3 2.5 fusion.23
  880.7 2.1 copy.223
  882.8 2.4 copy.190
  885.2 4.4 copy.224
  889.6 141.2 %reduce-scatter.16.cloned.1.call-done = bf16[64,2048]{1,0:T(8,128)(2,1)} async-done(((bf16[2048,2048]{1,0:T(8,128)(2,1)}), bf16[64,2048]{1,0:T(8,128)(2,1)}) %reduce-scatter.16.cloned.1.call-update) | async-done | bytes 262160 | tf_op jit(solution)/shard_map/reduce_scatter | solution.py:96
  1030.9 1.8 convert_element_type.144
  (148 shorter events, 21.7 us)
Async XLA Ops:
  7.2 92.4 %all-gather.10.cloned.1.call-start = ((), (), s32[]{:S(2)}) async-start(), calls=%async_computation.13 | async-start | bytes 3932160 | tf_op jit(solution)/shard_map/all_gather | solution.py:92
  8.5 29.2 %copy-start = (bf16[128,2048]{1,0:T(8,128)(2,1)S(1)}, bf16[128,2048]{1,0:T(8,128)(2,1)}, u32[]{:S(2)}) copy-start(bf16[128,2048]{1,0:T(8,128)(2,1)} %param.8) | copy-start | bytes 1572868
  8.7 32.1 %copy-start.11 = (bf16[64,16384]{1,0:T(8,128)(2,1)S(1)}, bf16[64,16384]{1,0:T(8,128)(2,1)}, u32[]{:S(2)}) copy-start(bf16[64,16384]{1,0:T(8,128)(2,1)} %param.11) | copy-start | bytes 6291460
  37.7 92.0 %all-gather.8.cloned.1.call-start = ((), (), s32[]{:S(2)}) async-start(), calls=%async_computation.12 | async-start | bytes 4718592 | tf_op jit(solution)/shard_map/all_gather | solution.py:92
  37.9 0.5 copy-start.16
  38.4 0.5 copy-start.18
  40.0 170.2 %all-gather.12.cloned.1.call-start = ((), (), s32[]{:S(2)}) async-start(), calls=%async_computation.14 | async-start | bytes 8650752 | tf_op jit(solution)/shard_map/all_gather | solution.py:92
  40.8 257.9 %all-gather.16.cloned.1.call-start = ((), (), s32[]{:S(2)}) async-start(), calls=%async_computation.16 | async-start | bytes 10485760 | tf_op jit(solution)/shard_map/all_gather | solution.py:92
  93.3 2.6 copy-start.21
  93.3 2.8 copy-start.20
  95.3 252.2 %all-gather.14.cloned.1.call-start = ((), (), s32[]{:S(2)}) async-start(), calls=%async_computation.15 | async-start | bytes 4718592 | tf_op jit(solution)/shard_map/all_gather | solution.py:92
  98.4 38.1 %copy-start.1 = (f32[1024,128]{0,1:T(8,128)}, f32[1024,128]{0,1:T(8,128)S(1)}, u32[]{:S(2)}) copy-start(f32[1024,128]{0,1:T(8,128)S(1)} %get-tuple-element.42) | copy-start | bytes 1572868
  98.4 38.1 %copy-start.4 = (f32[1024,128]{0,1:T(8,128)}, f32[1024,128]{0,1:T(8,128)S(1)}, u32[]{:S(2)}) copy-start(f32[1024,128]{0,1:T(8,128)S(1)} %get-tuple-element.41) | copy-start | bytes 1572868
  99.6 41.9 %copy-start.6 = (pred[1024,1024]{0,1:T(8,128)(4,1)}, pred[1024,1024]{0,1:T(8,128)(4,1)S(1)}, u32[]{:S(2)}) copy-start(pred[1024,1024]{0,1:T(8,128)(4,1)S(1)} %compare_and_fusion) | copy-start | bytes 3145732
  136.0 5.4 copy-start.14
  137.1 2.0 copy-start.8
  137.1 2.0 copy-start.12
  139.2 3.2 copy-start.3
  148.4 19.4 %collective-permute-start.5 = (bf16[1,128,256]{2,1,0:T(8,128)(2,1)S(1)}, bf16[1,128,256]{2,1,0:T(8,128)(2,1)S(1)}, u32[]{:S(2)}, u32[]{:S(2)}) collective-permute-start(bf16[1,128,256]{2,1,0:T(8,128)(2,1)S(1)} %bitcast.172), channel_id=1, source_target_pairs={{0,6},{1,7},{2,0},{3,1},{4,2},{5,3},{6,4},{7,5},{8,14},{9,15},{10,... | collective-permute-start | bytes 196616 | tf_op jit(solution)/shard_map/ppermute | solution.py:163
  149.9 5.7 collective-permute-start
  149.9 6.9 collective-permute-start.1
  150.5 17.2 %collective-permute-start.2 = (bf16[1,128,256]{2,1,0:T(8,128)(2,1)S(1)}, bf16[1,128,256]{2,1,0:T(8,128)(2,1)S(1)}, u32[]{:S(2)}, u32[]{:S(2)}) collective-permute-start(bf16[1,128,256]{2,1,0:T(8,128)(2,1)S(1)} %bitcast.174), channel_id=1, source_target_pairs={{0,3},{1,4},{2,5},{3,6},{4,7},{5,0},{6,1},{7,2},{8,11},{9,12},{10,... | collective-permute-start | bytes 196616 | tf_op jit(solution)/shard_map/ppermute | solution.py:163
  151.7 16.0 %collective-permute-start.3 = (bf16[1,128,256]{2,1,0:T(8,128)(2,1)S(1)}, bf16[1,128,256]{2,1,0:T(8,128)(2,1)S(1)}, u32[]{:S(2)}, u32[]{:S(2)}) collective-permute-start(bf16[1,128,256]{2,1,0:T(8,128)(2,1)S(1)} %bitcast.173), channel_id=1, source_target_pairs={{0,4},{1,5},{2,6},{3,7},{4,0},{5,1},{6,2},{7,3},{8,12},{9,13},{10,... | collective-permute-start | bytes 196616 | tf_op jit(solution)/shard_map/ppermute | solution.py:163
  155.5 12.3 %collective-permute-start.4 = (bf16[1,128,256]{2,1,0:T(8,128)(2,1)S(1)}, bf16[1,128,256]{2,1,0:T(8,128)(2,1)S(1)}, u32[]{:S(2)}, u32[]{:S(2)}) collective-permute-start(bf16[1,128,256]{2,1,0:T(8,128)(2,1)S(1)} %bitcast.171), channel_id=1, source_target_pairs={{0,5},{1,6},{2,7},{3,0},{4,1},{5,2},{6,3},{7,4},{8,13},{9,14},{10,... | collective-permute-start | bytes 196616 | tf_op jit(solution)/shard_map/ppermute | solution.py:163
  156.7 13.8 %collective-permute-start.6 = (bf16[1,128,256]{2,1,0:T(8,128)(2,1)S(1)}, bf16[1,128,256]{2,1,0:T(8,128)(2,1)S(1)}, u32[]{:S(2)}, u32[]{:S(2)}) collective-permute-start(bf16[1,128,256]{2,1,0:T(8,128)(2,1)S(1)} %bitcast.170), channel_id=1, source_target_pairs={{0,7},{1,0},{2,1},{3,2},{4,3},{5,4},{6,5},{7,6},{8,15},{9,8},{10,9... | collective-permute-start | bytes 196616 | tf_op jit(solution)/shard_map/ppermute | solution.py:163
  216.3 184.4 %all-gather.18.cloned.1.call-start = ((), (), s32[]{:S(2)}) async-start(), calls=%async_computation.17 | async-start | bytes 5242880 | tf_op jit(solution)/shard_map/all_gather | solution.py:92
  216.8 232.3 %all-gather.20.cloned.1.call-start = ((), (), s32[]{:S(2)}) async-start(), calls=%async_computation.19 | async-start | bytes 4718592 | tf_op jit(solution)/shard_map/all_gather | solution.py:92
  217.6 308.2 %reduce-scatter.10.cloned.1.call-start = ((), (), s32[]{:S(2)}) async-start(), calls=%async_computation.20 | async-start | bytes 4718592 | tf_op jit(solution)/shard_map/reduce_scatter | solution.py:96
  462.3 1.4 copy-start.24
  462.3 2.0 copy-start.25
  476.9 99.6 %reduce-scatter.8.cloned.1.call-start = ((), (), s32[]{:S(2)}) async-start(), calls=%async_computation.18 | async-start | bytes 4718592 | tf_op jit(solution)/shard_map/reduce_scatter | solution.py:96
  586.3 27.4 %copy-start.7 = (pred[1024,1024]{0,1:T(8,128)(4,1)S(1)}, pred[1024,1024]{0,1:T(8,128)(4,1)}, u32[]{:S(2)}) copy-start(pred[1024,1024]{0,1:T(8,128)(4,1)} %copy-done.6) | copy-start | bytes 3145732
  588.4 19.5 %all-to-all-start.2 = ((bf16[8,128,256]{1,2,0:T(8,128)(2,1)}), bf16[8,128,256]{1,2,0:T(8,128)(2,1)}, u32[]{:S(2)}, u32[]{:S(2)}) async-start(bf16[8,128,256]{1,2,0:T(8,128)(2,1)} %bitcast.157), calls=%async_computation.4 | async-start | bytes 1048576 | tf_op jit(solution)/shard_map/all_to_all | solution.py:194
  592.6 86.6 %reduce-scatter.14.cloned.1.call-start = ((), (), s32[]{:S(2)}) async-start(), calls=%async_computation.22 | async-start | bytes 3932160 | tf_op jit(solution)/shard_map/reduce_scatter | solution.py:96
  613.6 6.6 copy-start.10
  613.6 6.6 copy-start.15
  620.2 10.4 copy-start.23
  620.2 6.2 copy-start.13
  626.4 1.6 copy-start.2
  626.5 1.6 copy-start.9
  628.9 1.0 copy-start.5
  629.0 2.3 copy-start.22
  636.2 132.3 %reduce-scatter.18.cloned.1.call-start = ((), (), s32[]{:S(2)}) async-start(), calls=%async_computation.24 | async-start | bytes 10485760 | tf_op jit(solution)/shard_map/reduce_scatter | solution.py:96
  650.5 173.5 %reduce-scatter.20.cloned.1.call-start = ((), (), s32[]{:S(2)}) async-start(), calls=%async_computation.25 | async-start | bytes 5242880 | tf_op jit(solution)/shard_map/reduce_scatter | solution.py:96
  660.1 216.7 %reduce-scatter.12.cloned.1.call-start = ((), (), s32[]{:S(2)}) async-start(), calls=%async_computation.21 | async-start | bytes 4718592 | tf_op jit(solution)/shard_map/reduce_scatter | solution.py:96
  668.0 362.9 %reduce-scatter.16.cloned.1.call-start = ((), (), s32[]{:S(2)}) async-start(), calls=%async_computation.23 | async-start | bytes 8650752 | tf_op jit(solution)/shard_map/reduce_scatter | solution.py:96
  679.1 89.4 %all-to-all-start.3 = ((bf16[8,64,768]{2,1,0:T(8,128)(2,1)}), bf16[8,64,768]{2,1,0:T(8,128)(2,1)S(1)}, u32[]{:S(2)}, u32[]{:S(2)}) async-start(bf16[8,64,768]{2,1,0:T(8,128)(2,1)} %bitcast.161), calls=%async_computation.7 | async-start | bytes 1572864 | tf_op jit(solution)/shard_map/all_to_all | solution.py:111
  768.5 112.2 %all-to-all-start.4 = ((bf16[8,64,2048]{2,1,0:T(8,128)(2,1)}), bf16[8,64,2048]{2,1,0:T(8,128)(2,1)}, u32[]{:S(2)}, u32[]{:S(2)}) async-start(bf16[8,64,2048]{2,1,0:T(8,128)(2,1)} %bitcast.156), calls=%async_computation.10 | async-start | bytes 4194304 | tf_op jit(solution)/shard_map/all_to_all | solution.py:111
  826.8 50.0 %copy-start.17 = (f32[128]{0:T(128)S(1)}, f32[128]{0:T(128)}, u32[]{:S(2)}) copy-start(f32[128]{0:T(128)} %copy-done.16) | copy-start | bytes 1540
  826.8 50.0 %copy-start.19 = (f32[128]{0:T(128)S(1)}, f32[128]{0:T(128)}, u32[]{:S(2)}) copy-start(f32[128]{0:T(128)} %copy-done.18) | copy-start | bytes 1540
Sparse Core Ops, SparseCore 0:
  37.8 42.7 all-gather.9
  82.8 46.8 all-gather.7
  132.7 77.5 all-gather.11
  212.5 86.0 all-gather.15
  300.7 46.8 all-gather.13
  349.3 51.3 all-gather.17
  402.3 46.8 all-gather.19
  477.0 48.7 reduce-scatter.9
  528.1 48.3 reduce-scatter.7
  636.4 42.7 reduce-scatter.13
  682.2 86.2 reduce-scatter.17
  771.3 52.6 reduce-scatter.19
  826.9 49.8 reduce-scatter.11
  879.0 151.8 reduce-scatter.15
